TPU v7x, 256 devices: a whole 4x4x8 slice. The times are simulated.
256 devices in a mesh: leaf: 32 (over z, y), front: 8 (over x, core).
Axes of the slice: x: 4, y: 4, z: 8, core: 2. Of those that a mesh axis runs over, the one named last changes fastest.
Arguments:
- section_updates: bfloat16 [32768, 256], P(('leaf', 'front')), may hold values from -6 to 6
- upper_rhs: float32 [126976, 256], P(('leaf', 'front')), may hold values from -6 to 6
- pivot_inverse: bfloat16 [126976, 4096], P('leaf', 'front'), may hold values from -0.09375 to 0.09375
- coupling: bfloat16 [1024, 122880], P('front', 'leaf'), may hold values from -0.09375 to 0.09375
- extend_lists: int32 [62, 8], replicated, may hold values from 0 to 39, as said below
Outputs:
- solution: float32 [126976, 256], P(('leaf', 'front'))
- interface: bfloat16 [32768, 256], P(('leaf', 'front'))
Inputs may be any that keep to these rules, and one draw needn't show every extreme that they name: `extend_lists`: each row names 8 different blocks of the parent's frame; the rows of the root's two children name pivot blocks only, below 32.
All inputs are finite; a program needn't handle non-finite values.
Results may differ from a plain program's by a relative error of at most 0.022.
Values may be sent and summed in bfloat16 or wider, within the bound.
A program may use at most 64 MiB of HBM per device.

v0:
```python
import jax
import jax.numpy as jnp
from jax import lax
from jax.sharding import PartitionSpec as P

PIV = 4096
UPD = 1024
BLK = 128


def partner(block, axis, stride):
    count = lax.axis_size(axis)
    route = []
    for low in range(count):
        high = low | 1 << stride
        if high != low and high < count:
            route += [(low, high), (high, low)]
    return lax.ppermute(block, axis, route)


def child_base(leaves, height):
    total_rows = 0
    for depth in range(height - 1):
        total_rows = total_rows + leaves // 2**depth
    return total_rows


def list_row(extend_lists, row_index):
    return lax.dynamic_slice_in_dim(extend_lists, row_index, 1, 0)[0]


def upper_bit(position, bit_index):
    return position >> bit_index & 1 == 1


def joined(position, bit_index, portion, partner_rows):
    return jnp.where(
        upper_bit(position, bit_index),
        jnp.concatenate([partner_rows, portion], 0),
        jnp.concatenate([portion, partner_rows], 0),
    )


def gather_own(portion, height, position):
    for bit_index in range(height):
        partner_rows = partner(portion.astype(jnp.bfloat16), "leaf", bit_index).astype(
            portion.dtype
        )
        portion = joined(position, bit_index, portion, partner_rows)
    return portion


def sum_updates(summand, height):
    for bit_index in range(height):
        summand = summand + partner(summand.astype(jnp.bfloat16), "leaf", bit_index).astype(
            summand.dtype
        )
    return summand


def sum_solution(summand, height):
    for bit_index in range(height):
        summand = summand + partner(summand.astype(jnp.bfloat16), "leaf", bit_index).astype(
            summand.dtype
        )
    return summand


def front_sum(summand):
    bits = lax.axis_size("front").bit_length() - 1
    for bit_index in range(bits):
        half = summand.astype(jnp.bfloat16)
        summand = half.astype(jnp.float32) + partner(half, "front", bit_index).astype(jnp.float32)
    return summand


def per_device(section_updates, upper_rhs, pivot_inverse, coupling, extend_lists):
    leaves = lax.axis_size("leaf")
    fronts = lax.axis_size("front")
    levels = leaves.bit_length() - 1
    position = lax.axis_index("leaf")
    column = lax.axis_index("front")
    rhs_width = upper_rhs.shape[1]
    piv_dev = PIV // fronts
    upd_dev = UPD // fronts
    piv_blocks = piv_dev // BLK
    upd_blocks = upd_dev // BLK
    block_count = UPD // BLK
    local_blocks = jnp.concatenate(
        [
            column * piv_blocks + jnp.arange(piv_blocks, dtype=jnp.int32),
            PIV // BLK + column * upd_blocks + jnp.arange(upd_blocks, dtype=jnp.int32),
        ]
    )
    local_count = piv_blocks + upd_blocks
    carried = section_updates
    saved_part = []
    saved_half = []
    for height in range(1, levels + 1):
        group_size = 2**height
        span_rows = PIV // group_size
        band_start = PIV - PIV // 2 ** (height - 1)
        rhs_len = piv_dev // group_size
        rhs_start = piv_dev - piv_dev // 2 ** (height - 1)
        member = position & group_size - 1
        own_child = child_base(leaves, height) + (position >> height - 1)
        sibling = partner(carried, "leaf", height - 1)
        pair_blocks = lax.all_gather(jnp.stack([carried, sibling]), "front", axis=1, tiled=True)
        pair_lists = jnp.stack(
            [list_row(extend_lists, own_child), list_row(extend_lists, own_child ^ 1)]
        )
        chooser = (pair_lists.reshape(2 * block_count)[None, :] == local_blocks[:, None]).astype(
            jnp.bfloat16
        )
        assembled = jnp.dot(
            chooser,
            pair_blocks.reshape(2 * block_count, BLK * rhs_width),
            preferred_element_type=jnp.float32,
        ).reshape(local_count * BLK, rhs_width)
        own_rows = gather_own(upper_rhs[rhs_start : rhs_start + rhs_len], height, position)
        rows_half = (own_rows + assembled[:piv_dev]).astype(jnp.bfloat16)
        g_share = pivot_inverse[band_start : band_start + span_rows]
        pivot_part = front_sum(jnp.dot(g_share, rows_half, preferred_element_type=jnp.float32))
        pivot_half = pivot_part.astype(jnp.bfloat16)
        saved_part.append(pivot_part)
        saved_half.append(pivot_half)
        if height < levels:
            c_share = coupling[:, band_start : band_start + span_rows]
            summand = jnp.dot(c_share, pivot_half, preferred_element_type=jnp.float32)
            frame_upd = assembled[piv_dev:]
            carried = (frame_upd - sum_updates(summand, height)).astype(jnp.bfloat16)
    from_above = carried
    outputs = []
    for height in range(levels, 0, -1):
        group_size = 2**height
        span_rows = PIV // group_size
        band_start = PIV - PIV // 2 ** (height - 1)
        member = position & group_size - 1
        pivot_part = saved_part[height - 1]
        if height < levels:
            c_share = coupling[:, band_start : band_start + span_rows]
            back_total = front_sum(
                jnp.einsum("up,ur->pr", c_share, from_above, preferred_element_type=jnp.float32)
            )
            weight_half = (pivot_part - back_total).astype(jnp.bfloat16)
            upper_rows = from_above
        else:
            weight_half = saved_half[height - 1]
            upper_rows = jnp.zeros((upd_dev, rhs_width), jnp.bfloat16)
        g_share = pivot_inverse[band_start : band_start + span_rows]
        solve_term = jnp.einsum(
            "cp,cr->pr", g_share, weight_half, preferred_element_type=jnp.float32
        )
        part_len = piv_dev // group_size
        summed = sum_solution(solve_term, height)
        portion = lax.dynamic_slice_in_dim(summed, member * part_len, part_len, 0)
        rows_half = summed.astype(jnp.bfloat16)
        outputs.append(portion)
        frame_half = jnp.concatenate([rows_half, upper_rows], 0).reshape(
            local_count, BLK * rhs_width
        )
        child_list = list_row(extend_lists, child_base(leaves, height) + (position >> height - 1))
        picker = (child_list[:, None] == local_blocks[None, :]).astype(jnp.bfloat16)
        outgoing = (
            jnp.dot(picker, frame_half, preferred_element_type=jnp.float32)
            .astype(jnp.bfloat16)
            .reshape(fronts, upd_dev, rhs_width)
        )
        incoming = lax.all_to_all(outgoing, "front", split_axis=0, concat_axis=0, tiled=True)
        from_above = jnp.sum(incoming, axis=0, dtype=jnp.float32).astype(jnp.bfloat16)
    solution = jnp.concatenate(outputs[::-1], 0)
    return (solution, from_above)


def solution(mesh):
    placed = (
        P(("leaf", "front"), None),
        P(("leaf", "front"), None),
        P("leaf", "front"),
        P("front", "leaf"),
        P(),
    )
    return jax.shard_map(
        per_device,
        mesh=mesh,
        in_specs=placed,
        out_specs=(P(("leaf", "front"), None), P(("leaf", "front"), None)),
        check_vma=False,
    )
```

profile of v0, /device:TPU:24, one launch (start us, length us, event | category | flops | bytes accessed | tf_op | source)
XLA Modules:
  0.0 750.2 jit_solution(16977858934660072619)
XLA Ops:
  20.1 21.8 %all-gather.6.cloned.1.call-done = bf16[2,1024,256]{2,1,0:T(8,128)(2,1)} async-done(((bf16[2,128,256]{2,1,0:T(8,128)(2,1)}), bf16[2,1024,256]{2,1,0:T(8,128)(2,1)}) %all-gather.6.cloned.1.call-update) | async-done | bytes 1048592 | tf_op jit(solution)/shard_map/all_gather | solution.py:108
  50.2 25.3 %collective-permute-done.3 = bf16[2048,256]{0,1:T(8,128)(2,1)S(1)} collective-permute-done((bf16[2048,256]{0,1:T(8,128)(2,1)S(1)}, bf16[2048,256]{0,1:T(8,128)(2,1)S(1)}, u32[]{:S(2)}, u32[]{:S(2)}) %collective-permute-start.3) | collective-permute-done | bytes 1048608 | tf_op jit(solution)/shard_map/ppermute | solution.py:18
  77.7 24.3 %collective-permute-done.4 = bf16[2048,256]{0,1:T(8,128)(2,1)S(1)} collective-permute-done((bf16[2048,256]{0,1:T(8,128)(2,1)S(1)}, bf16[2048,256]{0,1:T(8,128)(2,1)S(1)}, u32[]{:S(2)}, u32[]{:S(2)}) %collective-permute-start.4) | collective-permute-done | bytes 1048608 | tf_op jit(solution)/shard_map/ppermute | solution.py:18
  126.5 13.9 %all-gather.8.cloned.1.call-done = bf16[2,1024,256]{1,2,0:T(8,128)(2,1)} async-done(((bf16[2,128,256]{1,2,0:T(8,128)(2,1)}), bf16[2,1024,256]{1,2,0:T(8,128)(2,1)}) %all-gather.8.cloned.1.call-update) | async-done | bytes 1048592 | tf_op jit(solution)/shard_map/all_gather | solution.py:108
  148.6 13.1 %collective-permute-done.10 = bf16[1024,256]{0,1:T(8,128)(2,1)S(1)} collective-permute-done((bf16[1024,256]{0,1:T(8,128)(2,1)S(1)}, bf16[1024,256]{0,1:T(8,128)(2,1)S(1)}, u32[]{:S(2)}, u32[]{:S(2)}) %collective-permute-start.10) | collective-permute-done | bytes 524320 | tf_op jit(solution)/shard_map/ppermute | solution.py:18
  164.7 12.0 %collective-permute-done.11 = bf16[1024,256]{0,1:T(8,128)(2,1)S(1)} collective-permute-done((bf16[1024,256]{0,1:T(8,128)(2,1)S(1)}, bf16[1024,256]{0,1:T(8,128)(2,1)S(1)}, u32[]{:S(2)}, u32[]{:S(2)}) %collective-permute-start.11) | collective-permute-done | bytes 524320 | tf_op jit(solution)/shard_map/ppermute | solution.py:18
  210.5 11.0 %all-gather.10.cloned.1.call-done = bf16[2,1024,256]{1,2,0:T(8,128)(2,1)} async-done(((bf16[2,128,256]{1,2,0:T(8,128)(2,1)}), bf16[2,1024,256]{1,2,0:T(8,128)(2,1)}) %all-gather.10.cloned.1.call-update) | async-done | bytes 1048592 | tf_op jit(solution)/shard_map/all_gather | solution.py:108
  429.0 13.4 %collective-permute-done.48 = bf16[512,256]{0,1:T(8,128)(2,1)S(1)} collective-permute-done((bf16[512,256]{0,1:T(8,128)(2,1)S(1)}, bf16[512,256]{0,1:T(8,128)(2,1)S(1)}, u32[]{:S(2)}, u32[]{:S(2)}) %collective-permute-start.48) | collective-permute-done | bytes 262176 | tf_op jit(solution)/shard_map/ppermute | solution.py:18
  447.9 7.8 %collective-permute-done.49 = bf16[512,256]{0,1:T(8,128)(2,1)S(1)} collective-permute-done((bf16[512,256]{0,1:T(8,128)(2,1)S(1)}, bf16[512,256]{0,1:T(8,128)(2,1)S(1)}, u32[]{:S(2)}, u32[]{:S(2)}) %collective-permute-start.49) | collective-permute-done | bytes 262176 | tf_op jit(solution)/shard_map/ppermute | solution.py:18
  457.6 14.1 %all_to_all.25 = bf16[8,128,256]{2,1,0:T(8,128)(2,1)S(1)} all-to-all(bf16[8,128,256]{2,1,0:T(8,128)(2,1)S(1)} %copy.50), channel_id=1, replica_groups=mesh['leaf'=32,'front'=8] {'front'}, dimensions={0} | all-to-all | bytes 1048576 | tf_op jit(solution)/shard_map/all_to_all | solution.py:169
  494.9 7.9 %collective-permute-done.54 = bf16[512,256]{0,1:T(8,128)(2,1)S(1)} collective-permute-done((bf16[512,256]{0,1:T(8,128)(2,1)S(1)}, bf16[512,256]{0,1:T(8,128)(2,1)S(1)}, u32[]{:S(2)}, u32[]{:S(2)}) %collective-permute-start.54) | collective-permute-done | bytes 262176 | tf_op jit(solution)/shard_map/ppermute | solution.py:18
  503.0 8.5 %collective-permute-done.55 = bf16[512,256]{0,1:T(8,128)(2,1)S(1)} collective-permute-done((bf16[512,256]{0,1:T(8,128)(2,1)S(1)}, bf16[512,256]{0,1:T(8,128)(2,1)S(1)}, u32[]{:S(2)}, u32[]{:S(2)}) %collective-permute-start.55) | collective-permute-done | bytes 262176 | tf_op jit(solution)/shard_map/ppermute | solution.py:18
  514.1 7.6 %collective-permute-done.56 = bf16[512,256]{0,1:T(8,128)(2,1)} collective-permute-done((bf16[512,256]{0,1:T(8,128)(2,1)}, bf16[512,256]{0,1:T(8,128)(2,1)}, u32[]{:S(2)}, u32[]{:S(2)}) %collective-permute-start.56) | collective-permute-done | bytes 262176 | tf_op jit(solution)/shard_map/ppermute | solution.py:18
  524.9 13.6 %all_to_all.26 = bf16[8,128,256]{2,1,0:T(8,128)(2,1)} all-to-all(bf16[8,128,256]{2,1,0:T(8,128)(2,1)S(1)} %copy.54), channel_id=1, replica_groups=mesh['leaf'=32,'front'=8] {'front'}, dimensions={0} | all-to-all | bytes 1048576 | tf_op jit(solution)/shard_map/all_to_all | solution.py:169
  542.2 7.8 %collective-permute-done.58 = bf16[512,256]{0,1:T(8,128)(2,1)S(1)} collective-permute-done((bf16[512,256]{0,1:T(8,128)(2,1)S(1)}, bf16[512,256]{0,1:T(8,128)(2,1)S(1)}, u32[]{:S(2)}, u32[]{:S(2)}) %collective-permute-start.58) | collective-permute-done | bytes 262176 | tf_op jit(solution)/shard_map/ppermute | solution.py:18
  551.0 8.1 %collective-permute-done.59 = bf16[512,256]{0,1:T(8,128)(2,1)S(1)} collective-permute-done((bf16[512,256]{0,1:T(8,128)(2,1)S(1)}, bf16[512,256]{0,1:T(8,128)(2,1)S(1)}, u32[]{:S(2)}, u32[]{:S(2)}) %collective-permute-start.59) | collective-permute-done | bytes 262176 | tf_op jit(solution)/shard_map/ppermute | solution.py:18
  568.3 7.9 %collective-permute-done.61 = bf16[512,256]{0,1:T(8,128)(2,1)S(1)} collective-permute-done((bf16[512,256]{0,1:T(8,128)(2,1)S(1)}, bf16[512,256]{0,1:T(8,128)(2,1)S(1)}, u32[]{:S(2)}, u32[]{:S(2)}) %collective-permute-start.61) | collective-permute-done | bytes 262176 | tf_op jit(solution)/shard_map/ppermute | solution.py:18
  587.4 12.8 %all_to_all.27 = bf16[8,128,256]{2,1,0:T(8,128)(2,1)S(1)} all-to-all(bf16[8,128,256]{2,1,0:T(8,128)(2,1)S(1)} %copy.58), channel_id=1, replica_groups=mesh['leaf'=32,'front'=8] {'front'}, dimensions={0} | all-to-all | bytes 1048576 | tf_op jit(solution)/shard_map/all_to_all | solution.py:169
  603.4 13.4 %collective-permute-done.64 = bf16[1024,256]{0,1:T(8,128)(2,1)S(1)} collective-permute-done((bf16[1024,256]{0,1:T(8,128)(2,1)S(1)}, bf16[1024,256]{0,1:T(8,128)(2,1)S(1)}, u32[]{:S(2)}, u32[]{:S(2)}) %collective-permute-start.64) | collective-permute-done | bytes 524320 | tf_op jit(solution)/shard_map/ppermute | solution.py:18
  618.0 13.7 %collective-permute-done.65 = bf16[1024,256]{0,1:T(8,128)(2,1)S(1)} collective-permute-done((bf16[1024,256]{0,1:T(8,128)(2,1)S(1)}, bf16[1024,256]{0,1:T(8,128)(2,1)S(1)}, u32[]{:S(2)}, u32[]{:S(2)}) %collective-permute-start.65) | collective-permute-done | bytes 524320 | tf_op jit(solution)/shard_map/ppermute | solution.py:18
  641.3 7.7 %collective-permute-done.67 = bf16[512,256]{0,1:T(8,128)(2,1)S(1)} collective-permute-done((bf16[512,256]{0,1:T(8,128)(2,1)S(1)}, bf16[512,256]{0,1:T(8,128)(2,1)S(1)}, u32[]{:S(2)}, u32[]{:S(2)}) %collective-permute-start.67) | collective-permute-done | bytes 262176 | tf_op jit(solution)/shard_map/ppermute | solution.py:18
  651.0 13.0 %all_to_all.28 = bf16[8,128,256]{2,1,0:T(8,128)(2,1)S(1)} all-to-all(bf16[8,128,256]{2,1,0:T(8,128)(2,1)S(1)} %copy.62), channel_id=1, replica_groups=mesh['leaf'=32,'front'=8] {'front'}, dimensions={0} | all-to-all | bytes 1048576 | tf_op jit(solution)/shard_map/all_to_all | solution.py:169
  668.3 24.6 %collective-permute-done.69 = bf16[2048,256]{0,1:T(8,128)(2,1)S(1)} collective-permute-done((bf16[2048,256]{0,1:T(8,128)(2,1)S(1)}, bf16[2048,256]{0,1:T(8,128)(2,1)S(1)}, u32[]{:S(2)}, u32[]{:S(2)}) %collective-permute-start.69) | collective-permute-done | bytes 1048608 | tf_op jit(solution)/shard_map/ppermute | solution.py:18
  694.3 25.0 %collective-permute-done.70 = bf16[2048,256]{0,1:T(8,128)(2,1)S(1)} collective-permute-done((bf16[2048,256]{0,1:T(8,128)(2,1)S(1)}, bf16[2048,256]{0,1:T(8,128)(2,1)S(1)}, u32[]{:S(2)}, u32[]{:S(2)}) %collective-permute-start.70) | collective-permute-done | bytes 1048608 | tf_op jit(solution)/shard_map/ppermute | solution.py:18
  (398 shorter events, 406.3 us)
Async XLA Ops:
  7.2 34.8 %all-gather.6.cloned.1.call-start = ((), (), s32[]{:S(2)}) async-start(), calls=%async_computation.5 | async-start | bytes 1179648 | tf_op jit(solution)/shard_map/all_gather | solution.py:108
  13.3 127.1 %all-gather.8.cloned.1.call-start = ((), (), s32[]{:S(2)}) async-start(), calls=%async_computation.6 | async-start | bytes 1179648 | tf_op jit(solution)/shard_map/all_gather | solution.py:108
  50.1 25.4 %collective-permute-start.3 = (bf16[2048,256]{0,1:T(8,128)(2,1)S(1)}, bf16[2048,256]{0,1:T(8,128)(2,1)S(1)}, u32[]{:S(2)}, u32[]{:S(2)}) collective-permute-start(bf16[2048,256]{0,1:T(8,128)(2,1)S(1)} %add_convert_fusion.3), channel_id=1, source_target_pairs={{0,2},{2,0},{1,3},{3,1},{4,6},{6,4},{5,7},{7,5},{8,10},{10,8},{9,1... | collective-permute-start | bytes 3145736 | tf_op jit(solution)/shard_map/ppermute | solution.py:18
  76.0 26.0 %collective-permute-start.4 = (bf16[2048,256]{0,1:T(8,128)(2,1)S(1)}, bf16[2048,256]{0,1:T(8,128)(2,1)S(1)}, u32[]{:S(2)}, u32[]{:S(2)}) collective-permute-start(bf16[2048,256]{0,1:T(8,128)(2,1)S(1)} %add_convert_fusion.2), channel_id=1, source_target_pairs={{0,4},{4,0},{1,5},{5,1},{2,6},{6,2},{3,7},{7,3},{8,12},{12,8},{9,1... | collective-permute-start | bytes 3145736 | tf_op jit(solution)/shard_map/ppermute | solution.py:18
  114.9 106.6 %all-gather.10.cloned.1.call-start = ((), (), s32[]{:S(2)}) async-start(), calls=%async_computation.7 | async-start | bytes 1179648 | tf_op jit(solution)/shard_map/all_gather | solution.py:108
  147.4 14.4 %collective-permute-start.10 = (bf16[1024,256]{0,1:T(8,128)(2,1)S(1)}, bf16[1024,256]{0,1:T(8,128)(2,1)S(1)}, u32[]{:S(2)}, u32[]{:S(2)}) collective-permute-start(bf16[1024,256]{0,1:T(8,128)(2,1)S(1)} %add_convert_fusion.7), channel_id=1, source_target_pairs={{0,2},{2,0},{1,3},{3,1},{4,6},{6,4},{5,7},{7,5},{8,10},{10,8},{9,1... | collective-permute-start | bytes 1572872 | tf_op jit(solution)/shard_map/ppermute | solution.py:18
  162.0 14.8 %collective-permute-start.11 = (bf16[1024,256]{0,1:T(8,128)(2,1)S(1)}, bf16[1024,256]{0,1:T(8,128)(2,1)S(1)}, u32[]{:S(2)}, u32[]{:S(2)}) collective-permute-start(bf16[1024,256]{0,1:T(8,128)(2,1)S(1)} %add_convert_fusion.6), channel_id=1, source_target_pairs={{0,4},{4,0},{1,5},{5,1},{2,6},{6,2},{3,7},{7,3},{8,12},{12,8},{9,1... | collective-permute-start | bytes 1572872 | tf_op jit(solution)/shard_map/ppermute | solution.py:18
  194.8 105.1 %all-gather.12.cloned.1.call-start = ((), (), s32[]{:S(2)}) async-start(), calls=%async_computation.8 | async-start | bytes 1179648 | tf_op jit(solution)/shard_map/all_gather | solution.py:108
  230.5 8.5 %collective-permute-start.19 = (bf16[512,256]{0,1:T(8,128)(2,1)S(1)}, bf16[512,256]{0,1:T(8,128)(2,1)S(1)}, u32[]{:S(2)}, u32[]{:S(2)}) collective-permute-start(bf16[512,256]{0,1:T(8,128)(2,1)S(1)} %add_convert_fusion.11), channel_id=1, source_target_pairs={{0,2},{2,0},{1,3},{3,1},{4,6},{6,4},{5,7},{7,5},{8,10},{10,8},{9,1... | collective-permute-start | bytes 786440 | tf_op jit(solution)/shard_map/ppermute | solution.py:18
  239.1 9.2 %collective-permute-start.20 = (bf16[512,256]{0,1:T(8,128)(2,1)S(1)}, bf16[512,256]{0,1:T(8,128)(2,1)S(1)}, u32[]{:S(2)}, u32[]{:S(2)}) collective-permute-start(bf16[512,256]{0,1:T(8,128)(2,1)S(1)} %add_convert_fusion.10), channel_id=1, source_target_pairs={{0,4},{4,0},{1,5},{5,1},{2,6},{6,2},{3,7},{7,3},{8,12},{12,8},{9,1... | collective-permute-start | bytes 786440 | tf_op jit(solution)/shard_map/ppermute | solution.py:18
  273.1 111.0 %all-gather.14.cloned.1.call-start = ((), (), s32[]{:S(2)}) async-start(), calls=%async_computation.9 | async-start | bytes 1179648 | tf_op jit(solution)/shard_map/all_gather | solution.py:108
  345.5 8.7 %collective-permute-start.41 = (bf16[128,256]{0,1:T(8,128)(2,1)S(1)}, bf16[128,256]{0,1:T(8,128)(2,1)S(1)}, u32[]{:S(2)}, u32[]{:S(2)}) collective-permute-start(bf16[128,256]{0,1:T(8,128)(2,1)S(1)} %subtract_convert_fusion.8), channel_id=1, source_target_pairs={{0,128},{128,0},{8,136},{136,8},{16,144},{144,16},{24,152},{152,24... | collective-permute-start | bytes 196616 | tf_op jit(solution)/shard_map/ppermute | solution.py:18
  374.1 9.8 %collective-permute-start.36 = (bf16[256,256]{1,0:T(8,128)(2,1)S(1)}, bf16[256,256]{1,0:T(8,128)(2,1)S(1)}, u32[]{:S(2)}, u32[]{:S(2)}) collective-permute-start(bf16[256,256]{1,0:T(8,128)(2,1)S(1)} %get-tuple-element.30), channel_id=1, source_target_pairs={{0,128},{128,0},{8,136},{136,8},{16,144},{144,16},{24,152},{152,24... | collective-permute-start | bytes 393224 | tf_op jit(solution)/shard_map/ppermute | solution.py:18
  426.6 15.8 %collective-permute-start.48 = (bf16[512,256]{0,1:T(8,128)(2,1)S(1)}, bf16[512,256]{0,1:T(8,128)(2,1)S(1)}, u32[]{:S(2)}, u32[]{:S(2)}) collective-permute-start(bf16[512,256]{0,1:T(8,128)(2,1)S(1)} %fusion.37), channel_id=1, source_target_pairs={{0,64},{64,0},{8,72},{72,8},{16,80},{80,16},{24,88},{88,24},{32,96... | collective-permute-start | bytes 786440 | tf_op jit(solution)/shard_map/ppermute | solution.py:18
  442.5 13.2 %collective-permute-start.49 = (bf16[512,256]{0,1:T(8,128)(2,1)S(1)}, bf16[512,256]{0,1:T(8,128)(2,1)S(1)}, u32[]{:S(2)}, u32[]{:S(2)}) collective-permute-start(bf16[512,256]{0,1:T(8,128)(2,1)S(1)} %fusion.58), channel_id=1, source_target_pairs={{0,128},{128,0},{8,136},{136,8},{16,144},{144,16},{24,152},{152,24... | collective-permute-start | bytes 786440 | tf_op jit(solution)/shard_map/ppermute | solution.py:18
  502.9 8.6 %collective-permute-start.55 = (bf16[512,256]{0,1:T(8,128)(2,1)S(1)}, bf16[512,256]{0,1:T(8,128)(2,1)S(1)}, u32[]{:S(2)}, u32[]{:S(2)}) collective-permute-start(bf16[512,256]{0,1:T(8,128)(2,1)S(1)} %fusion.111), channel_id=1, source_target_pairs={{0,32},{32,0},{8,40},{40,8},{16,48},{48,16},{24,56},{56,24},{64,96... | collective-permute-start | bytes 786440 | tf_op jit(solution)/shard_map/ppermute | solution.py:18
  512.3 9.4 %collective-permute-start.56 = (bf16[512,256]{0,1:T(8,128)(2,1)}, bf16[512,256]{0,1:T(8,128)(2,1)}, u32[]{:S(2)}, u32[]{:S(2)}) collective-permute-start(bf16[512,256]{0,1:T(8,128)(2,1)} %fusion.39), channel_id=1, source_target_pairs={{0,64},{64,0},{8,72},{72,8},{16,80},{80,16},{24,88},{88,24},{32,96... | collective-permute-start | bytes 786440 | tf_op jit(solution)/shard_map/ppermute | solution.py:18
  541.5 8.4 %collective-permute-start.58 = (bf16[512,256]{0,1:T(8,128)(2,1)S(1)}, bf16[512,256]{0,1:T(8,128)(2,1)S(1)}, u32[]{:S(2)}, u32[]{:S(2)}) collective-permute-start(bf16[512,256]{0,1:T(8,128)(2,1)S(1)} %add_convert_fusion.9), channel_id=1, source_target_pairs={{0,2},{2,0},{1,3},{3,1},{4,6},{6,4},{5,7},{7,5},{8,10},{10,8},{9,1... | collective-permute-start | bytes 786440 | tf_op jit(solution)/shard_map/ppermute | solution.py:18
  550.0 9.1 %collective-permute-start.59 = (bf16[512,256]{0,1:T(8,128)(2,1)S(1)}, bf16[512,256]{0,1:T(8,128)(2,1)S(1)}, u32[]{:S(2)}, u32[]{:S(2)}) collective-permute-start(bf16[512,256]{0,1:T(8,128)(2,1)S(1)} %add_convert_fusion.8), channel_id=1, source_target_pairs={{0,4},{4,0},{1,5},{5,1},{2,6},{6,2},{3,7},{7,3},{8,12},{12,8},{9,1... | collective-permute-start | bytes 786440 | tf_op jit(solution)/shard_map/ppermute | solution.py:18
  602.8 14.1 %collective-permute-start.64 = (bf16[1024,256]{0,1:T(8,128)(2,1)S(1)}, bf16[1024,256]{0,1:T(8,128)(2,1)S(1)}, u32[]{:S(2)}, u32[]{:S(2)}) collective-permute-start(bf16[1024,256]{0,1:T(8,128)(2,1)S(1)} %add_convert_fusion.5), channel_id=1, source_target_pairs={{0,2},{2,0},{1,3},{3,1},{4,6},{6,4},{5,7},{7,5},{8,10},{10,8},{9,1... | collective-permute-start | bytes 1572872 | tf_op jit(solution)/shard_map/ppermute | solution.py:18
  617.0 14.7 %collective-permute-start.65 = (bf16[1024,256]{0,1:T(8,128)(2,1)S(1)}, bf16[1024,256]{0,1:T(8,128)(2,1)S(1)}, u32[]{:S(2)}, u32[]{:S(2)}) collective-permute-start(bf16[1024,256]{0,1:T(8,128)(2,1)S(1)} %add_convert_fusion.4), channel_id=1, source_target_pairs={{0,4},{4,0},{1,5},{5,1},{2,6},{6,2},{3,7},{7,3},{8,12},{12,8},{9,1... | collective-permute-start | bytes 1572872 | tf_op jit(solution)/shard_map/ppermute | solution.py:18
  667.7 25.3 %collective-permute-start.69 = (bf16[2048,256]{0,1:T(8,128)(2,1)S(1)}, bf16[2048,256]{0,1:T(8,128)(2,1)S(1)}, u32[]{:S(2)}, u32[]{:S(2)}) collective-permute-start(bf16[2048,256]{0,1:T(8,128)(2,1)S(1)} %add_convert_fusion.1), channel_id=1, source_target_pairs={{0,2},{2,0},{1,3},{3,1},{4,6},{6,4},{5,7},{7,5},{8,10},{10,8},{9,1... | collective-permute-start | bytes 3145736 | tf_op jit(solution)/shard_map/ppermute | solution.py:18
  693.4 25.9 %collective-permute-start.70 = (bf16[2048,256]{0,1:T(8,128)(2,1)S(1)}, bf16[2048,256]{0,1:T(8,128)(2,1)S(1)}, u32[]{:S(2)}, u32[]{:S(2)}) collective-permute-start(bf16[2048,256]{0,1:T(8,128)(2,1)S(1)} %add_convert_fusion), channel_id=1, source_target_pairs={{0,4},{4,0},{1,5},{5,1},{2,6},{6,2},{3,7},{7,3},{8,12},{12,8},{9,1... | collective-permute-start | bytes 3145736 | tf_op jit(solution)/shard_map/ppermute | solution.py:18
  728.7 13.7 %all-to-all-start.4 = ((bf16[8,128,256]{2,1,0:T(8,128)(2,1)}), bf16[8,128,256]{2,1,0:T(8,128)(2,1)S(1)}, u32[]{:S(2)}, u32[]{:S(2)}) async-start(bf16[8,128,256]{2,1,0:T(8,128)(2,1)} %copy.66), calls=%async_computation.4 | async-start | bytes 1048576 | tf_op jit(solution)/shard_map/all_to_all | solution.py:169
  (88 other events, 1259.2 us)
Sparse Core Ops, SparseCore 0:
  13.4 28.4 all-gather.5
  115.0 25.4 all-gather.7
  194.9 26.4 all-gather.9
  273.2 26.6 all-gather.11
  355.1 26.6 all-gather.13
where the time goes:
time: 760 us; the launch traced here: 750 us
  waiting for transfers between devices  503 us (66%)
  starting transfers between devices  86.8 us (11%)
  blocking collectives  53.4 us (7%)
  local copies, waits for them, and re-layouts  38.9 us (5%)
  matrix products  26.4 us (3%)
  other arithmetic  25.6 us (3%)
  between operations  15.6 us (2%)
    ppermute x72, waiting for transfers between devices, partner(): return lax.ppermute(block, axis, route)  446 us
    ppermute x72, starting transfers between devices, partner(): return lax.ppermute(block, axis, route)  83.1 us
    all_to_all x4, blocking collectives, per_device(): lax.all_to_all(outgoing, 'front', split_axis=0, concat_axis=0, tiled=True)  53.4 us
    all_gather x5, waiting for transfers between devices, per_device(): lax.all_gather(jnp.stack([carried, sibling]), 'front', axis=1, tiled=True)  51.3 us
  transfers between devices with their start and end apart: 78, of which 77 were waited for; matrix products, arithmetic and copies ran while one was open for 3% of the time, Pallas kernels for 0%

commit v1 on v0

--- a/solution.py
+++ b/solution.py
@@ -105,7 +105,11 @@
         member = position & group_size - 1
         own_child = child_base(leaves, height) + (position >> height - 1)
         sibling = partner(carried, "leaf", height - 1)
-        pair_blocks = lax.all_gather(jnp.stack([carried, sibling]), "front", axis=1, tiled=True)
+        load = jnp.stack([carried, sibling])
+        pair_blocks = jnp.concatenate(
+            lax.all_to_all(jnp.stack([load for _ in range(lax.psum(1, "front"))]), "front", 0, 0),
+            axis=1,
+        )
         pair_lists = jnp.stack(
             [list_row(extend_lists, own_child), list_row(extend_lists, own_child ^ 1)]
         )

time: 760 us -> 724 us (0.953)
  waiting for transfers between devices: 503 us -> 474 us
  starting transfers between devices: 86.8 us -> 107 us
  between operations: 15.6 us -> 2.24 us
    all_gather x5 -> x0, waiting for transfers between devices: 51.3 us -> none  [per_device(): lax.all_gather(jnp.stack([carried, sibling]), 'front', axis=1, tiled=True)]
    all_to_all x0 -> x5, starting transfers between devices: none -> 21.2 us  [per_device(): lax.all_to_all(jnp.stack([load for _ in range(lax.psum(1, 'front'))]), 'f...]
    all_to_all x0 -> x5, waiting for transfers between devices: none -> 14.2 us  [per_device(): lax.all_to_all(jnp.stack([load for _ in range(lax.psum(1, 'front'))]), 'f...]
  transfers between devices with their start and end apart: 78 -> 78, of which waited for: 77 -> 76; matrix products, arithmetic and copies ran while one was open for 3% -> 2% of each run, Pallas kernels for 0% -> 0%
where the time goes in v1:
time: 724 us; the launch traced here: 715 us
  waiting for transfers between devices  474 us (65%)
  starting transfers between devices  107 us (15%)
  blocking collectives  53.8 us (7%)
  local copies, waits for them, and re-layouts  36.1 us (5%)
  matrix products  23.6 us (3%)
  other arithmetic  18.1 us (3%)
    ppermute x72, waiting for transfers between devices, partner(): return lax.ppermute(block, axis, route)  453 us
    ppermute x72, starting transfers between devices, partner(): return lax.ppermute(block, axis, route)  82.4 us
    all_to_all x4, blocking collectives, per_device(): lax.all_to_all(outgoing, 'front', split_axis=0, concat_axis=0, tiled=True)  53.8 us
    all_to_all x5, starting transfers between devices, per_device(): lax.all_to_all(jnp.stack([load for _ in range(lax.psum(1, 'front'))]), 'f...  21.2 us
  transfers between devices with their start and end apart: 78, of which 76 were waited for; matrix products, arithmetic and copies ran while one was open for 2% of the time, Pallas kernels for 0%

profile of v1, /device:TPU:24, one launch (start us, length us, event | category | flops | bytes accessed | tf_op | source)
XLA Modules:
  0.0 714.6 jit_solution(16496262088969836819)
XLA Ops:
  17.5 9.9 %all-to-all-done = bf16[8,2,128,256]{3,2,1,0:T(8,128)(2,1)S(1)} async-done(((bf16[8,2,128,256]{3,2,1,0:T(8,128)(2,1)}), bf16[8,2,128,256]{3,2,1,0:T(8,128)(2,1)S(1)}, u32[]{:S(2)}, u32[]{:S(2)}) %all-to-all-start) | async-done | bytes 1048608 | tf_op jit(solution)/shard_map/all_to_all | solution.py:110
  35.2 24.6 %collective-permute-done.3 = bf16[2048,256]{0,1:T(8,128)(2,1)S(1)} collective-permute-done((bf16[2048,256]{0,1:T(8,128)(2,1)S(1)}, bf16[2048,256]{0,1:T(8,128)(2,1)S(1)}, u32[]{:S(2)}, u32[]{:S(2)}) %collective-permute-start.3) | collective-permute-done | bytes 1048608 | tf_op jit(solution)/shard_map/ppermute | solution.py:18
  61.2 25.0 %collective-permute-done.4 = bf16[2048,256]{0,1:T(8,128)(2,1)S(1)} collective-permute-done((bf16[2048,256]{0,1:T(8,128)(2,1)S(1)}, bf16[2048,256]{0,1:T(8,128)(2,1)S(1)}, u32[]{:S(2)}, u32[]{:S(2)}) %collective-permute-start.4) | collective-permute-done | bytes 1048608 | tf_op jit(solution)/shard_map/ppermute | solution.py:18
  125.6 13.4 %collective-permute-done.10 = bf16[1024,256]{0,1:T(8,128)(2,1)S(1)} collective-permute-done((bf16[1024,256]{0,1:T(8,128)(2,1)S(1)}, bf16[1024,256]{0,1:T(8,128)(2,1)S(1)}, u32[]{:S(2)}, u32[]{:S(2)}) %collective-permute-start.10) | collective-permute-done | bytes 524320 | tf_op jit(solution)/shard_map/ppermute | solution.py:18
  140.2 13.7 %collective-permute-done.11 = bf16[1024,256]{0,1:T(8,128)(2,1)S(1)} collective-permute-done((bf16[1024,256]{0,1:T(8,128)(2,1)S(1)}, bf16[1024,256]{0,1:T(8,128)(2,1)S(1)}, u32[]{:S(2)}, u32[]{:S(2)}) %collective-permute-start.11) | collective-permute-done | bytes 524320 | tf_op jit(solution)/shard_map/ppermute | solution.py:18
  305.6 7.9 %collective-permute-start.41 = (bf16[128,256]{0,1:T(8,128)(2,1)S(1)}, bf16[128,256]{0,1:T(8,128)(2,1)S(1)}, u32[]{:S(2)}, u32[]{:S(2)}) collective-permute-start(bf16[128,256]{0,1:T(8,128)(2,1)S(1)} %subtract_convert_fusion.8), channel_id=1, source_target_pairs={{0,128},{128,0},{8,136},{136,8},{16,144},{144,16},{24,152},{152,24... | collective-permute-start | bytes 196616 | tf_op jit(solution)/shard_map/ppermute | solution.py:18
  374.7 7.9 %collective-permute-done.46 = bf16[512,256]{0,1:T(8,128)(2,1)S(1)} collective-permute-done((bf16[512,256]{0,1:T(8,128)(2,1)S(1)}, bf16[512,256]{0,1:T(8,128)(2,1)S(1)}, u32[]{:S(2)}, u32[]{:S(2)}) %collective-permute-start.46) | collective-permute-done | bytes 262176 | tf_op jit(solution)/shard_map/ppermute | solution.py:18
  382.8 8.3 %collective-permute-done.47 = bf16[512,256]{0,1:T(8,128)(2,1)S(1)} collective-permute-done((bf16[512,256]{0,1:T(8,128)(2,1)S(1)}, bf16[512,256]{0,1:T(8,128)(2,1)S(1)}, u32[]{:S(2)}, u32[]{:S(2)}) %collective-permute-start.47) | collective-permute-done | bytes 262176 | tf_op jit(solution)/shard_map/ppermute | solution.py:18
  391.6 15.2 %collective-permute-done.48 = bf16[512,256]{0,1:T(8,128)(2,1)S(1)} collective-permute-done((bf16[512,256]{0,1:T(8,128)(2,1)S(1)}, bf16[512,256]{0,1:T(8,128)(2,1)S(1)}, u32[]{:S(2)}, u32[]{:S(2)}) %collective-permute-start.48) | collective-permute-done | bytes 262176 | tf_op jit(solution)/shard_map/ppermute | solution.py:18
  412.3 7.8 %collective-permute-done.49 = bf16[512,256]{0,1:T(8,128)(2,1)S(1)} collective-permute-done((bf16[512,256]{0,1:T(8,128)(2,1)S(1)}, bf16[512,256]{0,1:T(8,128)(2,1)S(1)}, u32[]{:S(2)}, u32[]{:S(2)}) %collective-permute-start.49) | collective-permute-done | bytes 262176 | tf_op jit(solution)/shard_map/ppermute | solution.py:18
  423.8 15.3 %all_to_all.50 = bf16[8,128,256]{2,1,0:T(8,128)(2,1)S(1)} all-to-all(bf16[8,128,256]{2,1,0:T(8,128)(2,1)S(1)} %copy.59), channel_id=1, replica_groups=mesh['leaf'=32,'front'=8] {'front'}, dimensions={0} | all-to-all | bytes 1048576 | tf_op jit(solution)/shard_map/all_to_all | solution.py:173
  462.1 7.9 %collective-permute-done.54 = bf16[512,256]{0,1:T(8,128)(2,1)S(1)} collective-permute-done((bf16[512,256]{0,1:T(8,128)(2,1)S(1)}, bf16[512,256]{0,1:T(8,128)(2,1)S(1)}, u32[]{:S(2)}, u32[]{:S(2)}) %collective-permute-start.54) | collective-permute-done | bytes 262176 | tf_op jit(solution)/shard_map/ppermute | solution.py:18
  470.6 8.3 %collective-permute-done.55 = bf16[512,256]{0,1:T(8,128)(2,1)S(1)} collective-permute-done((bf16[512,256]{0,1:T(8,128)(2,1)S(1)}, bf16[512,256]{0,1:T(8,128)(2,1)S(1)}, u32[]{:S(2)}, u32[]{:S(2)}) %collective-permute-start.55) | collective-permute-done | bytes 262176 | tf_op jit(solution)/shard_map/ppermute | solution.py:18
  480.5 9.2 %collective-permute-done.56 = bf16[512,256]{0,1:T(8,128)(2,1)} collective-permute-done((bf16[512,256]{0,1:T(8,128)(2,1)}, bf16[512,256]{0,1:T(8,128)(2,1)}, u32[]{:S(2)}, u32[]{:S(2)}) %collective-permute-start.56) | collective-permute-done | bytes 262176 | tf_op jit(solution)/shard_map/ppermute | solution.py:18
  494.6 12.9 %all_to_all.51 = bf16[8,128,256]{2,1,0:T(8,128)(2,1)S(1)} all-to-all(bf16[8,128,256]{2,1,0:T(8,128)(2,1)S(1)} %copy.63), channel_id=1, replica_groups=mesh['leaf'=32,'front'=8] {'front'}, dimensions={0} | all-to-all | bytes 1048576 | tf_op jit(solution)/shard_map/all_to_all | solution.py:173
  519.0 8.1 %collective-permute-done.59 = bf16[512,256]{0,1:T(8,128)(2,1)S(1)} collective-permute-done((bf16[512,256]{0,1:T(8,128)(2,1)S(1)}, bf16[512,256]{0,1:T(8,128)(2,1)S(1)}, u32[]{:S(2)}, u32[]{:S(2)}) %collective-permute-start.59) | collective-permute-done | bytes 262176 | tf_op jit(solution)/shard_map/ppermute | solution.py:18
  536.2 7.9 %collective-permute-done.61 = bf16[512,256]{0,1:T(8,128)(2,1)S(1)} collective-permute-done((bf16[512,256]{0,1:T(8,128)(2,1)S(1)}, bf16[512,256]{0,1:T(8,128)(2,1)S(1)}, u32[]{:S(2)}, u32[]{:S(2)}) %collective-permute-start.61) | collective-permute-done | bytes 262176 | tf_op jit(solution)/shard_map/ppermute | solution.py:18
  557.0 12.8 %all_to_all.52 = bf16[8,128,256]{2,1,0:T(8,128)(2,1)S(1)} all-to-all(bf16[8,128,256]{2,1,0:T(8,128)(2,1)S(1)} %copy.67), channel_id=1, replica_groups=mesh['leaf'=32,'front'=8] {'front'}, dimensions={0} | all-to-all | bytes 1048576 | tf_op jit(solution)/shard_map/all_to_all | solution.py:173
  573.0 13.4 %collective-permute-done.64 = bf16[1024,256]{0,1:T(8,128)(2,1)S(1)} collective-permute-done((bf16[1024,256]{0,1:T(8,128)(2,1)S(1)}, bf16[1024,256]{0,1:T(8,128)(2,1)S(1)}, u32[]{:S(2)}, u32[]{:S(2)}) %collective-permute-start.64) | collective-permute-done | bytes 524320 | tf_op jit(solution)/shard_map/ppermute | solution.py:18
  587.6 13.7 %collective-permute-done.65 = bf16[1024,256]{0,1:T(8,128)(2,1)S(1)} collective-permute-done((bf16[1024,256]{0,1:T(8,128)(2,1)S(1)}, bf16[1024,256]{0,1:T(8,128)(2,1)S(1)}, u32[]{:S(2)}, u32[]{:S(2)}) %collective-permute-start.65) | collective-permute-done | bytes 524320 | tf_op jit(solution)/shard_map/ppermute | solution.py:18
  610.8 8.0 %collective-permute-done.67 = bf16[512,256]{0,1:T(8,128)(2,1)S(1)} collective-permute-done((bf16[512,256]{0,1:T(8,128)(2,1)}, bf16[512,256]{0,1:T(8,128)(2,1)S(1)}, u32[]{:S(2)}, u32[]{:S(2)}) %collective-permute-start.67) | collective-permute-done | bytes 262176 | tf_op jit(solution)/shard_map/ppermute | solution.py:18
  622.3 12.9 %all_to_all.53 = bf16[8,128,256]{2,1,0:T(8,128)(2,1)S(1)} all-to-all(bf16[8,128,256]{2,1,0:T(8,128)(2,1)S(1)} %copy.71), channel_id=1, replica_groups=mesh['leaf'=32,'front'=8] {'front'}, dimensions={0} | all-to-all | bytes 1048576 | tf_op jit(solution)/shard_map/all_to_all | solution.py:173
  639.6 24.6 %collective-permute-done.69 = bf16[2048,256]{0,1:T(8,128)(2,1)S(1)} collective-permute-done((bf16[2048,256]{0,1:T(8,128)(2,1)S(1)}, bf16[2048,256]{0,1:T(8,128)(2,1)S(1)}, u32[]{:S(2)}, u32[]{:S(2)}) %collective-permute-start.69) | collective-permute-done | bytes 1048608 | tf_op jit(solution)/shard_map/ppermute | solution.py:18
  665.6 25.0 %collective-permute-done.70 = bf16[2048,256]{0,1:T(8,128)(2,1)S(1)} collective-permute-done((bf16[2048,256]{0,1:T(8,128)(2,1)S(1)}, bf16[2048,256]{0,1:T(8,128)(2,1)S(1)}, u32[]{:S(2)}, u32[]{:S(2)}) %collective-permute-start.70) | collective-permute-done | bytes 1048608 | tf_op jit(solution)/shard_map/ppermute | solution.py:18
  (395 shorter events, 398.7 us)
Async XLA Ops:
  7.1 20.2 %all-to-all-start = ((bf16[8,2,128,256]{3,2,1,0:T(8,128)(2,1)}), bf16[8,2,128,256]{3,2,1,0:T(8,128)(2,1)S(1)}, u32[]{:S(2)}, u32[]{:S(2)}) async-start(bf16[8,2,128,256]{3,2,1,0:T(8,128)(2,1)} %stack.54), calls=%async_computation | async-start | bytes 2097152 | tf_op jit(solution)/shard_map/all_to_all | solution.py:110
  34.5 25.3 %collective-permute-start.3 = (bf16[2048,256]{0,1:T(8,128)(2,1)S(1)}, bf16[2048,256]{0,1:T(8,128)(2,1)S(1)}, u32[]{:S(2)}, u32[]{:S(2)}) collective-permute-start(bf16[2048,256]{0,1:T(8,128)(2,1)S(1)} %add_convert_fusion.3), channel_id=1, source_target_pairs={{0,2},{2,0},{1,3},{3,1},{4,6},{6,4},{5,7},{7,5},{8,10},{10,8},{9,1... | collective-permute-start | bytes 3145736 | tf_op jit(solution)/shard_map/ppermute | solution.py:18
  60.2 25.9 %collective-permute-start.4 = (bf16[2048,256]{0,1:T(8,128)(2,1)S(1)}, bf16[2048,256]{0,1:T(8,128)(2,1)S(1)}, u32[]{:S(2)}, u32[]{:S(2)}) collective-permute-start(bf16[2048,256]{0,1:T(8,128)(2,1)S(1)} %add_convert_fusion.2), channel_id=1, source_target_pairs={{0,4},{4,0},{1,5},{5,1},{2,6},{6,2},{3,7},{7,3},{8,12},{12,8},{9,1... | collective-permute-start | bytes 3145736 | tf_op jit(solution)/shard_map/ppermute | solution.py:18
  98.5 19.4 %all-to-all-start.1 = ((bf16[8,2,128,256]{3,2,1,0:T(8,128)(2,1)}), bf16[8,2,128,256]{3,2,1,0:T(8,128)(2,1)S(1)}, u32[]{:S(2)}, u32[]{:S(2)}) async-start(bf16[8,2,128,256]{3,2,1,0:T(8,128)(2,1)} %stack.59), calls=%async_computation.1 | async-start | bytes 2097152 | tf_op jit(solution)/shard_map/all_to_all | solution.py:110
  125.0 14.1 %collective-permute-start.10 = (bf16[1024,256]{0,1:T(8,128)(2,1)S(1)}, bf16[1024,256]{0,1:T(8,128)(2,1)S(1)}, u32[]{:S(2)}, u32[]{:S(2)}) collective-permute-start(bf16[1024,256]{0,1:T(8,128)(2,1)S(1)} %add_convert_fusion.7), channel_id=1, source_target_pairs={{0,2},{2,0},{1,3},{3,1},{4,6},{6,4},{5,7},{7,5},{8,10},{10,8},{9,1... | collective-permute-start | bytes 1572872 | tf_op jit(solution)/shard_map/ppermute | solution.py:18
  139.2 14.7 %collective-permute-start.11 = (bf16[1024,256]{0,1:T(8,128)(2,1)S(1)}, bf16[1024,256]{0,1:T(8,128)(2,1)S(1)}, u32[]{:S(2)}, u32[]{:S(2)}) collective-permute-start(bf16[1024,256]{0,1:T(8,128)(2,1)S(1)} %add_convert_fusion.6), channel_id=1, source_target_pairs={{0,4},{4,0},{1,5},{5,1},{2,6},{6,2},{3,7},{7,3},{8,12},{12,8},{9,1... | collective-permute-start | bytes 1572872 | tf_op jit(solution)/shard_map/ppermute | solution.py:18
  173.5 19.4 %all-to-all-start.2 = ((bf16[8,2,128,256]{3,2,1,0:T(8,128)(2,1)}), bf16[8,2,128,256]{3,2,1,0:T(8,128)(2,1)S(1)}, u32[]{:S(2)}, u32[]{:S(2)}) async-start(bf16[8,2,128,256]{3,2,1,0:T(8,128)(2,1)} %stack.64), calls=%async_computation.2 | async-start | bytes 2097152 | tf_op jit(solution)/shard_map/all_to_all | solution.py:110
  198.7 8.4 %collective-permute-start.19 = (bf16[512,256]{0,1:T(8,128)(2,1)S(1)}, bf16[512,256]{0,1:T(8,128)(2,1)S(1)}, u32[]{:S(2)}, u32[]{:S(2)}) collective-permute-start(bf16[512,256]{0,1:T(8,128)(2,1)S(1)} %add_convert_fusion.11), channel_id=1, source_target_pairs={{0,2},{2,0},{1,3},{3,1},{4,6},{6,4},{5,7},{7,5},{8,10},{10,8},{9,1... | collective-permute-start | bytes 786440 | tf_op jit(solution)/shard_map/ppermute | solution.py:18
  207.2 9.1 %collective-permute-start.20 = (bf16[512,256]{0,1:T(8,128)(2,1)S(1)}, bf16[512,256]{0,1:T(8,128)(2,1)S(1)}, u32[]{:S(2)}, u32[]{:S(2)}) collective-permute-start(bf16[512,256]{0,1:T(8,128)(2,1)S(1)} %add_convert_fusion.10), channel_id=1, source_target_pairs={{0,4},{4,0},{1,5},{5,1},{2,6},{6,2},{3,7},{7,3},{8,12},{12,8},{9,1... | collective-permute-start | bytes 786440 | tf_op jit(solution)/shard_map/ppermute | solution.py:18
  239.9 24.9 %all-to-all-start.3 = ((bf16[8,2,128,256]{3,2,1,0:T(8,128)(2,1)}), bf16[8,2,128,256]{3,2,1,0:T(8,128)(2,1)S(1)}, u32[]{:S(2)}, u32[]{:S(2)}) async-start(bf16[8,2,128,256]{3,2,1,0:T(8,128)(2,1)} %stack.134), calls=%async_computation.3 | async-start | bytes 2097152 | tf_op jit(solution)/shard_map/all_to_all | solution.py:110
  305.6 10.1 %collective-permute-start.41 = (bf16[128,256]{0,1:T(8,128)(2,1)S(1)}, bf16[128,256]{0,1:T(8,128)(2,1)S(1)}, u32[]{:S(2)}, u32[]{:S(2)}) collective-permute-start(bf16[128,256]{0,1:T(8,128)(2,1)S(1)} %subtract_convert_fusion.8), channel_id=1, source_target_pairs={{0,128},{128,0},{8,136},{136,8},{16,144},{144,16},{24,152},{152,24... | collective-permute-start | bytes 196616 | tf_op jit(solution)/shard_map/ppermute | solution.py:18
  317.0 33.4 %all-to-all-start.4 = ((bf16[8,2,128,256]{3,2,1,0:T(8,128)(2,1)}), bf16[8,2,128,256]{3,2,1,0:T(8,128)(2,1)S(1)}, u32[]{:S(2)}, u32[]{:S(2)}) async-start(bf16[8,2,128,256]{3,2,1,0:T(8,128)(2,1)} %stack.139), calls=%async_computation.4 | async-start | bytes 2097152 | tf_op jit(solution)/shard_map/all_to_all | solution.py:110
  341.4 9.0 %collective-permute-start.36 = (bf16[256,256]{1,0:T(8,128)(2,1)S(1)}, bf16[256,256]{1,0:T(8,128)(2,1)S(1)}, u32[]{:S(2)}, u32[]{:S(2)}) collective-permute-start(bf16[256,256]{1,0:T(8,128)(2,1)S(1)} %get-tuple-element.30), channel_id=1, source_target_pairs={{0,128},{128,0},{8,136},{136,8},{16,144},{144,16},{24,152},{152,24... | collective-permute-start | bytes 393224 | tf_op jit(solution)/shard_map/ppermute | solution.py:18
  382.7 8.4 %collective-permute-start.47 = (bf16[512,256]{0,1:T(8,128)(2,1)S(1)}, bf16[512,256]{0,1:T(8,128)(2,1)S(1)}, u32[]{:S(2)}, u32[]{:S(2)}) collective-permute-start(bf16[512,256]{0,1:T(8,128)(2,1)S(1)} %get-tuple-element.28), channel_id=1, source_target_pairs={{0,32},{32,0},{8,40},{40,8},{16,48},{48,16},{24,56},{56,24},{64,96... | collective-permute-start | bytes 786440 | tf_op jit(solution)/shard_map/ppermute | solution.py:18
  391.2 15.6 %collective-permute-start.48 = (bf16[512,256]{0,1:T(8,128)(2,1)S(1)}, bf16[512,256]{0,1:T(8,128)(2,1)S(1)}, u32[]{:S(2)}, u32[]{:S(2)}) collective-permute-start(bf16[512,256]{0,1:T(8,128)(2,1)S(1)} %fusion.37), channel_id=1, source_target_pairs={{0,64},{64,0},{8,72},{72,8},{16,80},{80,16},{24,88},{88,24},{32,96... | collective-permute-start | bytes 786440 | tf_op jit(solution)/shard_map/ppermute | solution.py:18
  406.9 13.2 %collective-permute-start.49 = (bf16[512,256]{0,1:T(8,128)(2,1)S(1)}, bf16[512,256]{0,1:T(8,128)(2,1)S(1)}, u32[]{:S(2)}, u32[]{:S(2)}) collective-permute-start(bf16[512,256]{0,1:T(8,128)(2,1)S(1)} %fusion.58), channel_id=1, source_target_pairs={{0,128},{128,0},{8,136},{136,8},{16,144},{144,16},{24,152},{152,24... | collective-permute-start | bytes 786440 | tf_op jit(solution)/shard_map/ppermute | solution.py:18
  470.1 8.8 %collective-permute-start.55 = (bf16[512,256]{0,1:T(8,128)(2,1)S(1)}, bf16[512,256]{0,1:T(8,128)(2,1)S(1)}, u32[]{:S(2)}, u32[]{:S(2)}) collective-permute-start(bf16[512,256]{0,1:T(8,128)(2,1)S(1)} %fusion.111), channel_id=1, source_target_pairs={{0,32},{32,0},{8,40},{40,8},{16,48},{48,16},{24,56},{56,24},{64,96... | collective-permute-start | bytes 786440 | tf_op jit(solution)/shard_map/ppermute | solution.py:18
  479.7 10.0 %collective-permute-start.56 = (bf16[512,256]{0,1:T(8,128)(2,1)}, bf16[512,256]{0,1:T(8,128)(2,1)}, u32[]{:S(2)}, u32[]{:S(2)}) collective-permute-start(bf16[512,256]{0,1:T(8,128)(2,1)} %fusion.39), channel_id=1, source_target_pairs={{0,64},{64,0},{8,72},{72,8},{16,80},{80,16},{24,88},{88,24},{32,96... | collective-permute-start | bytes 786440 | tf_op jit(solution)/shard_map/ppermute | solution.py:18
  518.0 9.1 %collective-permute-start.59 = (bf16[512,256]{0,1:T(8,128)(2,1)S(1)}, bf16[512,256]{0,1:T(8,128)(2,1)S(1)}, u32[]{:S(2)}, u32[]{:S(2)}) collective-permute-start(bf16[512,256]{0,1:T(8,128)(2,1)S(1)} %add_convert_fusion.8), channel_id=1, source_target_pairs={{0,4},{4,0},{1,5},{5,1},{2,6},{6,2},{3,7},{7,3},{8,12},{12,8},{9,1... | collective-permute-start | bytes 786440 | tf_op jit(solution)/shard_map/ppermute | solution.py:18
  572.3 14.1 %collective-permute-start.64 = (bf16[1024,256]{0,1:T(8,128)(2,1)S(1)}, bf16[1024,256]{0,1:T(8,128)(2,1)S(1)}, u32[]{:S(2)}, u32[]{:S(2)}) collective-permute-start(bf16[1024,256]{0,1:T(8,128)(2,1)S(1)} %add_convert_fusion.5), channel_id=1, source_target_pairs={{0,2},{2,0},{1,3},{3,1},{4,6},{6,4},{5,7},{7,5},{8,10},{10,8},{9,1... | collective-permute-start | bytes 1572872 | tf_op jit(solution)/shard_map/ppermute | solution.py:18
  586.6 14.7 %collective-permute-start.65 = (bf16[1024,256]{0,1:T(8,128)(2,1)S(1)}, bf16[1024,256]{0,1:T(8,128)(2,1)S(1)}, u32[]{:S(2)}, u32[]{:S(2)}) collective-permute-start(bf16[1024,256]{0,1:T(8,128)(2,1)S(1)} %add_convert_fusion.4), channel_id=1, source_target_pairs={{0,4},{4,0},{1,5},{5,1},{2,6},{6,2},{3,7},{7,3},{8,12},{12,8},{9,1... | collective-permute-start | bytes 1572872 | tf_op jit(solution)/shard_map/ppermute | solution.py:18
  638.9 25.3 %collective-permute-start.69 = (bf16[2048,256]{0,1:T(8,128)(2,1)S(1)}, bf16[2048,256]{0,1:T(8,128)(2,1)S(1)}, u32[]{:S(2)}, u32[]{:S(2)}) collective-permute-start(bf16[2048,256]{0,1:T(8,128)(2,1)S(1)} %add_convert_fusion.1), channel_id=1, source_target_pairs={{0,2},{2,0},{1,3},{3,1},{4,6},{6,4},{5,7},{7,5},{8,10},{10,8},{9,1... | collective-permute-start | bytes 3145736 | tf_op jit(solution)/shard_map/ppermute | solution.py:18
  664.6 25.9 %collective-permute-start.70 = (bf16[2048,256]{0,1:T(8,128)(2,1)S(1)}, bf16[2048,256]{0,1:T(8,128)(2,1)S(1)}, u32[]{:S(2)}, u32[]{:S(2)}) collective-permute-start(bf16[2048,256]{0,1:T(8,128)(2,1)S(1)} %add_convert_fusion), channel_id=1, source_target_pairs={{0,4},{4,0},{1,5},{5,1},{2,6},{6,2},{3,7},{7,3},{8,12},{12,8},{9,1... | collective-permute-start | bytes 3145736 | tf_op jit(solution)/shard_map/ppermute | solution.py:18
  700.0 13.7 %all-to-all-start.9 = ((bf16[8,128,256]{2,1,0:T(8,128)(2,1)}), bf16[8,128,256]{2,1,0:T(8,128)(2,1)S(1)}, u32[]{:S(2)}, u32[]{:S(2)}) async-start(bf16[8,128,256]{2,1,0:T(8,128)(2,1)} %copy.75), calls=%async_computation.9 | async-start | bytes 1048576 | tf_op jit(solution)/shard_map/all_to_all | solution.py:173
  (84 other events, 766.5 us)
